TPU v7x, 32 devices: a whole 2x2x4 slice. The times are simulated.
32 devices in a mesh: don: 4 (over x, core), acc: 8 (over z, y).
Axes of the slice: x: 2, y: 2, z: 4, core: 2. Of those that a mesh axis runs over, the one named last changes fastest.
Arguments:
- donor_emb: bfloat16 [65536, 768], P(('don', 'acc')), may hold values from -12 to 12
- acceptor_emb: bfloat16 [65536, 768], P(('don', 'acc')), may hold values from -6 to 6
- donor_pos: int32 [768], P(('don', 'acc')), may hold values from 0 to 2047
- acceptor_pos: int32 [768], P(('don', 'acc')), may hold values from 0 to 2047
- donor_count: int32 [32], P('don'), may hold values from 1 to 24, as said below
- acceptor_count: int32 [32], replicated, may hold values from 1 to 24, as said below
- target: int32 [64, 768], P(None, 'don'), may hold values from 0 to 767, as said below
- junction_mask: int32 [64, 768], P(None, 'don'), may hold values 0 or 1
- weights: bfloat16 [64, 768, 768], P('acc'), may hold values from -1 to 2
Outputs:
- loss: float32 [], replicated
- grad_weight: float32 [768, 64, 768], P('don', 'acc')
Inputs may be any that keep to these rules, and one draw needn't show every extreme that they name: `donor_count`: the live donor slots of all shards number exactly 400; some shard has all 24 live. `acceptor_count`: the live acceptor slots of all shards number exactly 400; some shard has all 24 live. `target`: each entry names a live acceptor slot.
All inputs are finite; a program needn't handle non-finite values. No bound on the sum of `junction_mask` on one device may be relied on, other than what follows from the above.
Results may differ from a plain program's by a relative error of at most 0.0031.
Values may be sent and summed in bfloat16 or wider, within the bound.
A program may use at most 128 MiB of HBM per device.

v0:
```python
import jax
import jax.numpy as jnp
from jax import lax
from jax.sharding import PartitionSpec as P


def local(
    donor_emb,
    acceptor_emb,
    donor_pos,
    acceptor_pos,
    donor_count,
    acceptor_count,
    target,
    junction_mask,
    weights,
):
    slots = donor_pos.shape[0]
    width = weights.shape[1]
    tis_dev = weights.shape[0]
    scale = width ** (-0.5)
    column = lax.axis_index("acc")
    donor_local = jnp.take(donor_emb, donor_pos, axis=0)
    acceptor_local = jnp.take(acceptor_emb, acceptor_pos, axis=0)
    donors = lax.all_gather(donor_local, "acc", axis=0, tiled=True)
    acceptors = lax.all_gather(acceptor_local, ("don", "acc"), axis=0, tiled=True)
    donor_rows = donors.shape[0]
    acceptor_rows = acceptors.shape[0]
    live_d = jnp.arange(donor_rows, dtype=jnp.int32) % slots < jnp.repeat(donor_count, slots)
    live_a = jnp.arange(acceptor_rows, dtype=jnp.int32) % slots < jnp.repeat(acceptor_count, slots)
    first_tissue = column * tis_dev
    targets_dev = lax.dynamic_slice_in_dim(target, first_tissue, tis_dev, 0)
    masks_dev = lax.dynamic_slice_in_dim(junction_mask, first_tissue, tis_dev, 0)
    weighting = jnp.where(live_d[None, :], masks_dev, 0).astype(jnp.float32)
    columns = jnp.arange(acceptor_rows, dtype=jnp.int32)

    def tissue(inputs):
        matrix, target_row, weight_row = inputs
        projected = jnp.dot(donors, matrix, preferred_element_type=jnp.float32).astype(jnp.bfloat16)
        scores = (
            lax.dot_general(
                projected, acceptors, (((1,), (1,)), ((), ())), preferred_element_type=jnp.float32
            )
            * scale
        )
        scores = jnp.where(live_a[None, :], scores, -1e30)
        highest = jnp.max(scores, axis=1, keepdims=True)
        summed_exp = jnp.sum(
            jnp.where(live_a[None, :], jnp.exp(scores - highest), 0.0), axis=1, keepdims=True
        )
        log_total = highest + jnp.log(summed_exp)
        is_target = columns[None, :] == target_row[:, None]
        picked = jnp.sum(jnp.where(is_target, scores, 0.0), axis=1)
        summed = jnp.sum(weight_row * (log_total[:, 0] - picked))
        counted = jnp.sum(weight_row)
        probs = jnp.where(live_a[None, :], jnp.exp(scores - log_total), 0.0)
        dscore = (weight_row[:, None] * (probs - is_target.astype(jnp.float32))).astype(
            jnp.bfloat16
        )
        dproj = (jnp.dot(dscore, acceptors, preferred_element_type=jnp.float32) * scale).astype(
            jnp.bfloat16
        )
        return (summed, counted, dproj)

    summed, counted, dproj = lax.map(tissue, (weights, targets_dev, weighting))
    summed, counted = lax.psum((jnp.sum(summed), jnp.sum(counted)), ("don", "acc"))
    loss = summed / jnp.maximum(counted, 1.0)
    donor_columns = lax.all_to_all(donors, "don", split_axis=1, concat_axis=0, tiled=True)
    grad_weight = jnp.einsum(
        "nd,tne->dte",
        donor_columns,
        lax.all_gather(dproj, "don", axis=1, tiled=True),
        preferred_element_type=jnp.float32,
    )
    return (loss, grad_weight)


def solution(mesh):
    return jax.shard_map(
        local,
        mesh=mesh,
        in_specs=(
            P(("don", "acc"), None),
            P(("don", "acc"), None),
            P(("don", "acc")),
            P(("don", "acc")),
            P("don"),
            P(),
            P(None, "don"),
            P(None, "don"),
            P("acc", None, None),
        ),
        out_specs=(P(), P("don", "acc", None)),
        check_vma=False,
    )
```

profile of v0, /device:TPU:0, one launch (start us, length us, event | category | flops | bytes accessed | tf_op | source)
XLA Modules:
  0.0 240.2 jit_solution(6414580511166542491)
XLA Ops:
  11.3 2.9 %gather_fusion = bf16[24,768]{1,0:T(8,128)(2,1)S(1)} fusion(bf16[2048,768]{1,0:T(8,128)(2,1)} %param.13, s32[1024]{0:T(1024)S(1)} %pad_clamp_fusion.1), kind=kCustom, calls=%fused_computation.clone | custom fusion | bytes 73824 | tf_op jit(solution)/shard_map/jit(_take)/gather | solution.py:23
  14.3 32.6 %all_gather.9 = bf16[192,768]{1,0:T(8,128)(2,1)S(1)} all-gather(bf16[24,768]{1,0:T(8,128)(2,1)S(1)} %broadcast_select_fusion.1), channel_id=1, replica_groups=mesh['don'=4,'acc'=8] {'acc'}, dimensions={0}, use_global_device_ids=true | all-gather | bytes 331776 | tf_op jit(solution)/shard_map/all_gather | solution.py:25
  47.7 20.0 %all-gather.3.cloned.1.call-done = bf16[768,768]{1,0:T(8,128)(2,1)} async-done(((bf16[24,768]{1,0:T(8,128)(2,1)}), bf16[768,768]{1,0:T(8,128)(2,1)}) %all-gather.3.cloned.1.call-update) | async-done | bytes 1179664 | tf_op jit(solution)/shard_map/all_gather | solution.py:26
  67.7 88.2 %while.15 = (s32[]{:T(128)}, f32[8]{0:T(128)S(1)}, f32[8]{0:T(128)S(1)}, bf16[8,192,768]{2,1,0:T(8,128)(2,1)}, f32[8,192]{1,0:T(8,128)S(1)}, /*index=5*/bf16[8,7...) while((s32[]{:T(128)}, f32[8]{0:T(128)S(1)}, ...), condition=%wide.region_6.8_spmd.clone, body=%wide.region_0.7_spmd.clone.sunk | while | flops 682284672 | bytes 5926949 | solution.py:65
  70.0 3.3 %fusion.59 = (f32[192]{0:T(256)S(1)}, f32[192,768]{1,0:T(8,128)}) fusion(bf16[768,768]{1,0:T(8,128)(2,1)} %get-tuple-element.237, bf16[192,768]{1,0:T(8,128)(2,1)S(1)} %get-tuple-element.236, bf16[8,768,768]{2,1,0:T(8,128)(2,1)} %get-tuple-element.235, s32[]{:T(128)S(6)} %copy.26, pred[768]{0:T(1024)(128)(4,1)S(1)} %fusion.58), kind=kOutput, calls=%fused_computation.51.clone.1 | convolution fusion | flops 453574464 | bytes 3245572 | tf_op jit(solution)/shard_map/while/body/eval_jaxpr/dot_general | solution.py:41
  73.3 1.4 fusion.60
  76.1 2.7 %fusion.61 = bf16[8,192,768]{2,1,0:T(8,128)(2,1)} fusion(bf16[8,192,768]{2,1,0:T(8,128)(2,1)} %get-tuple-element.222, s32[]{:T(128)S(6)} %copy.26, bf16[768,768]{1,0:T(8,128)(2,1)} %get-tuple-element.237, f32[192,768]{1,0:T(8,128)} %get-tuple-element.201, f32[192]{0:T(256)S(1)} %get-tuple-element.207, f32[192]{0:T(256)S(1)} %bitcast.47, ...), kind=kOutput, calls=%fused_computation.12.clone.1 | convolution fusion | flops 227819520 | bytes 2067460 | tf_op jit(solution)/shard_map/while/body/eval_jaxpr/dot_general | solution.py:60
  81.0 3.3 %fusion.59 = (f32[192]{0:T(256)S(1)}, f32[192,768]{1,0:T(8,128)}) fusion(bf16[768,768]{1,0:T(8,128)(2,1)} %get-tuple-element.237, bf16[192,768]{1,0:T(8,128)(2,1)S(1)} %get-tuple-element.236, bf16[8,768,768]{2,1,0:T(8,128)(2,1)} %get-tuple-element.235, s32[]{:T(128)S(6)} %copy.26, pred[768]{0:T(1024)(128)(4,1)S(1)} %fusion.58), kind=kOutput, calls=%fused_computation.51.clone.1 | convolution fusion | flops 453574464 | bytes 3245572 | tf_op jit(solution)/shard_map/while/body/eval_jaxpr/dot_general | solution.py:41
  84.3 1.4 fusion.60
  87.1 2.7 %fusion.61 = bf16[8,192,768]{2,1,0:T(8,128)(2,1)} fusion(bf16[8,192,768]{2,1,0:T(8,128)(2,1)} %get-tuple-element.222, s32[]{:T(128)S(6)} %copy.26, bf16[768,768]{1,0:T(8,128)(2,1)} %get-tuple-element.237, f32[192,768]{1,0:T(8,128)} %get-tuple-element.201, f32[192]{0:T(256)S(1)} %get-tuple-element.207, f32[192]{0:T(256)S(1)} %bitcast.47, ...), kind=kOutput, calls=%fused_computation.12.clone.1 | convolution fusion | flops 227819520 | bytes 2067460 | tf_op jit(solution)/shard_map/while/body/eval_jaxpr/dot_general | solution.py:60
  92.0 3.3 %fusion.59 = (f32[192]{0:T(256)S(1)}, f32[192,768]{1,0:T(8,128)}) fusion(bf16[768,768]{1,0:T(8,128)(2,1)} %get-tuple-element.237, bf16[192,768]{1,0:T(8,128)(2,1)S(1)} %get-tuple-element.236, bf16[8,768,768]{2,1,0:T(8,128)(2,1)} %get-tuple-element.235, s32[]{:T(128)S(6)} %copy.26, pred[768]{0:T(1024)(128)(4,1)S(1)} %fusion.58), kind=kOutput, calls=%fused_computation.51.clone.1 | convolution fusion | flops 453574464 | bytes 3245572 | tf_op jit(solution)/shard_map/while/body/eval_jaxpr/dot_general | solution.py:41
  95.4 1.4 fusion.60
  98.1 2.7 %fusion.61 = bf16[8,192,768]{2,1,0:T(8,128)(2,1)} fusion(bf16[8,192,768]{2,1,0:T(8,128)(2,1)} %get-tuple-element.222, s32[]{:T(128)S(6)} %copy.26, bf16[768,768]{1,0:T(8,128)(2,1)} %get-tuple-element.237, f32[192,768]{1,0:T(8,128)} %get-tuple-element.201, f32[192]{0:T(256)S(1)} %get-tuple-element.207, f32[192]{0:T(256)S(1)} %bitcast.47, ...), kind=kOutput, calls=%fused_computation.12.clone.1 | convolution fusion | flops 227819520 | bytes 2067460 | tf_op jit(solution)/shard_map/while/body/eval_jaxpr/dot_general | solution.py:60
  103.0 3.3 %fusion.59 = (f32[192]{0:T(256)S(1)}, f32[192,768]{1,0:T(8,128)}) fusion(bf16[768,768]{1,0:T(8,128)(2,1)} %get-tuple-element.237, bf16[192,768]{1,0:T(8,128)(2,1)S(1)} %get-tuple-element.236, bf16[8,768,768]{2,1,0:T(8,128)(2,1)} %get-tuple-element.235, s32[]{:T(128)S(6)} %copy.26, pred[768]{0:T(1024)(128)(4,1)S(1)} %fusion.58), kind=kOutput, calls=%fused_computation.51.clone.1 | convolution fusion | flops 453574464 | bytes 3245572 | tf_op jit(solution)/shard_map/while/body/eval_jaxpr/dot_general | solution.py:41
  106.4 1.4 fusion.60
  109.2 2.7 %fusion.61 = bf16[8,192,768]{2,1,0:T(8,128)(2,1)} fusion(bf16[8,192,768]{2,1,0:T(8,128)(2,1)} %get-tuple-element.222, s32[]{:T(128)S(6)} %copy.26, bf16[768,768]{1,0:T(8,128)(2,1)} %get-tuple-element.237, f32[192,768]{1,0:T(8,128)} %get-tuple-element.201, f32[192]{0:T(256)S(1)} %get-tuple-element.207, f32[192]{0:T(256)S(1)} %bitcast.47, ...), kind=kOutput, calls=%fused_computation.12.clone.1 | convolution fusion | flops 227819520 | bytes 2067460 | tf_op jit(solution)/shard_map/while/body/eval_jaxpr/dot_general | solution.py:60
  114.1 3.3 %fusion.59 = (f32[192]{0:T(256)S(1)}, f32[192,768]{1,0:T(8,128)}) fusion(bf16[768,768]{1,0:T(8,128)(2,1)} %get-tuple-element.237, bf16[192,768]{1,0:T(8,128)(2,1)S(1)} %get-tuple-element.236, bf16[8,768,768]{2,1,0:T(8,128)(2,1)} %get-tuple-element.235, s32[]{:T(128)S(6)} %copy.26, pred[768]{0:T(1024)(128)(4,1)S(1)} %fusion.58), kind=kOutput, calls=%fused_computation.51.clone.1 | convolution fusion | flops 453574464 | bytes 3245572 | tf_op jit(solution)/shard_map/while/body/eval_jaxpr/dot_general | solution.py:41
  117.4 1.4 fusion.60
  120.2 2.7 %fusion.61 = bf16[8,192,768]{2,1,0:T(8,128)(2,1)} fusion(bf16[8,192,768]{2,1,0:T(8,128)(2,1)} %get-tuple-element.222, s32[]{:T(128)S(6)} %copy.26, bf16[768,768]{1,0:T(8,128)(2,1)} %get-tuple-element.237, f32[192,768]{1,0:T(8,128)} %get-tuple-element.201, f32[192]{0:T(256)S(1)} %get-tuple-element.207, f32[192]{0:T(256)S(1)} %bitcast.47, ...), kind=kOutput, calls=%fused_computation.12.clone.1 | convolution fusion | flops 227819520 | bytes 2067460 | tf_op jit(solution)/shard_map/while/body/eval_jaxpr/dot_general | solution.py:60
  125.1 3.3 %fusion.59 = (f32[192]{0:T(256)S(1)}, f32[192,768]{1,0:T(8,128)}) fusion(bf16[768,768]{1,0:T(8,128)(2,1)} %get-tuple-element.237, bf16[192,768]{1,0:T(8,128)(2,1)S(1)} %get-tuple-element.236, bf16[8,768,768]{2,1,0:T(8,128)(2,1)} %get-tuple-element.235, s32[]{:T(128)S(6)} %copy.26, pred[768]{0:T(1024)(128)(4,1)S(1)} %fusion.58), kind=kOutput, calls=%fused_computation.51.clone.1 | convolution fusion | flops 453574464 | bytes 3245572 | tf_op jit(solution)/shard_map/while/body/eval_jaxpr/dot_general | solution.py:41
  128.4 1.4 fusion.60
  131.2 2.7 %fusion.61 = bf16[8,192,768]{2,1,0:T(8,128)(2,1)} fusion(bf16[8,192,768]{2,1,0:T(8,128)(2,1)} %get-tuple-element.222, s32[]{:T(128)S(6)} %copy.26, bf16[768,768]{1,0:T(8,128)(2,1)} %get-tuple-element.237, f32[192,768]{1,0:T(8,128)} %get-tuple-element.201, f32[192]{0:T(256)S(1)} %get-tuple-element.207, f32[192]{0:T(256)S(1)} %bitcast.47, ...), kind=kOutput, calls=%fused_computation.12.clone.1 | convolution fusion | flops 227819520 | bytes 2067460 | tf_op jit(solution)/shard_map/while/body/eval_jaxpr/dot_general | solution.py:60
  136.1 3.3 %fusion.59 = (f32[192]{0:T(256)S(1)}, f32[192,768]{1,0:T(8,128)}) fusion(bf16[768,768]{1,0:T(8,128)(2,1)} %get-tuple-element.237, bf16[192,768]{1,0:T(8,128)(2,1)S(1)} %get-tuple-element.236, bf16[8,768,768]{2,1,0:T(8,128)(2,1)} %get-tuple-element.235, s32[]{:T(128)S(6)} %copy.26, pred[768]{0:T(1024)(128)(4,1)S(1)} %fusion.58), kind=kOutput, calls=%fused_computation.51.clone.1 | convolution fusion | flops 453574464 | bytes 3245572 | tf_op jit(solution)/shard_map/while/body/eval_jaxpr/dot_general | solution.py:41
  139.5 1.4 fusion.60
  142.2 2.7 %fusion.61 = bf16[8,192,768]{2,1,0:T(8,128)(2,1)} fusion(bf16[8,192,768]{2,1,0:T(8,128)(2,1)} %get-tuple-element.222, s32[]{:T(128)S(6)} %copy.26, bf16[768,768]{1,0:T(8,128)(2,1)} %get-tuple-element.237, f32[192,768]{1,0:T(8,128)} %get-tuple-element.201, f32[192]{0:T(256)S(1)} %get-tuple-element.207, f32[192]{0:T(256)S(1)} %bitcast.47, ...), kind=kOutput, calls=%fused_computation.12.clone.1 | convolution fusion | flops 227819520 | bytes 2067460 | tf_op jit(solution)/shard_map/while/body/eval_jaxpr/dot_general | solution.py:60
  147.1 3.3 %fusion.59 = (f32[192]{0:T(256)S(1)}, f32[192,768]{1,0:T(8,128)}) fusion(bf16[768,768]{1,0:T(8,128)(2,1)} %get-tuple-element.237, bf16[192,768]{1,0:T(8,128)(2,1)S(1)} %get-tuple-element.236, bf16[8,768,768]{2,1,0:T(8,128)(2,1)} %get-tuple-element.235, s32[]{:T(128)S(6)} %copy.26, pred[768]{0:T(1024)(128)(4,1)S(1)} %fusion.58), kind=kOutput, calls=%fused_computation.51.clone.1 | convolution fusion | flops 453574464 | bytes 3245572 | tf_op jit(solution)/shard_map/while/body/eval_jaxpr/dot_general | solution.py:41
  153.2 2.7 %fusion.61 = bf16[8,192,768]{2,1,0:T(8,128)(2,1)} fusion(bf16[8,192,768]{2,1,0:T(8,128)(2,1)} %get-tuple-element.222, s32[]{:T(128)S(6)} %copy.26, bf16[768,768]{1,0:T(8,128)(2,1)} %get-tuple-element.237, f32[192,768]{1,0:T(8,128)} %get-tuple-element.201, f32[192]{0:T(256)S(1)} %get-tuple-element.207, f32[192]{0:T(256)S(1)} %bitcast.47, ...), kind=kOutput, calls=%fused_computation.12.clone.1 | convolution fusion | flops 227819520 | bytes 2067460 | tf_op jit(solution)/shard_map/while/body/eval_jaxpr/dot_general | solution.py:60
  157.8 10.2 %all_to_all.19 = bf16[192,4,192]{0,2,1:T(8,128)(2,1)S(1)} all-to-all(bf16[192,4,192]{0,2,1:T(8,128)(2,1)S(1)} %bitcast.43), channel_id=1, replica_groups=mesh['don'=4,'acc'=8] {'don'}, dimensions={1} | all-to-all | bytes 589824 | tf_op jit(solution)/shard_map/all_to_all | solution.py:68
  170.5 39.5 %all-reduce = (f32[]{:T(128)}, f32[]{:T(128)}) all-reduce(f32[]{:T(128)} %reduce_sum.54, f32[]{:T(128)} %reduce_sum.55), channel_id=1, replica_groups=mesh['don'=4,'acc'=8] {'don','acc'}, use_global_device_ids=true, to_apply=%region_8.10 | all-reduce | flops 2 | bytes 16 | tf_op jit(solution)/shard_map/psum | solution.py:66
  211.2 10.4 %all-gather.5.cloned.1.call-done = bf16[8,768,768]{2,1,0:T(8,128)(2,1)} async-done(((bf16[8,192,768]{2,1,0:T(8,128)(2,1)}), bf16[8,768,768]{2,1,0:T(8,128)(2,1)}) %all-gather.5.cloned.1.call-update) | async-done | bytes 9437200 | tf_op jit(solution)/shard_map/all_gather | solution.py:72
  221.6 5.8 %fusion.36 = f32[192,8,768]{2,0,1:T(8,128)S(1)} fusion(bf16[768,192,1]{0,1,2:T(8,128)(2,1)} %reshape.75, bf16[8,768,768]{2,1,0:T(8,128)(2,1)} %all-gather.5.cloned.1.call-done), kind=kOutput, calls=%fused_computation.52 | convolution fusion | flops 1811939328 | bytes 14450688 | tf_op jit(solution)/shard_map/nd,tne->dte/dot_general | solution.py:69
  227.4 4.9 %copy.17 = f32[192,8,768]{2,1,0:T(8,128)} copy(f32[192,8,768]{2,0,1:T(8,128)S(1)} %fusion.36) | data formatting | bytes 9437184
  (92 shorter events, 39.5 us)
Async XLA Ops:
  7.2 1.9 copy-start
  7.2 60.6 %all-gather.3.cloned.1.call-start = ((), (), s32[]{:S(2)}) async-start(), calls=%async_computation.1 | async-start | bytes 1216512 | tf_op jit(solution)/shard_map/all_gather | solution.py:26
  10.4 211.1 %all-gather.5.cloned.1.call-start = ((), (), s32[]{:S(2)}) async-start(), calls=%async_computation.2 | async-start | bytes 11796480 | tf_op jit(solution)/shard_map/all_gather | solution.py:72
  155.9 0.7 copy-start.1
Sparse Core Ops, SparseCore 0:
  10.9 56.7 all-gather.2
  156.8 64.7 all-gather.4
where the time goes:
time: 242 us; the launch traced here: 240 us
  blocking collectives  82.3 us (34%)
  matrix products  54 us (22%)
  local copies, waits for them, and re-layouts  31 us (13%)
  waiting for transfers between devices  30.5 us (13%)
  other arithmetic  25.9 us (11%)
  between operations  16.4 us (7%)
    psum x1, blocking collectives, local(): lax.psum((jnp.sum(summed), jnp.sum(counted)), ('don', 'acc'))  39.5 us
    all_gather x1, blocking collectives, local(): donors = lax.all_gather(donor_local, 'acc', axis=0, tiled=True)  32.6 us
    dot_general x8, matrix products, tissue(): lax.dot_general(projected, acceptors, (((1,), (1,)), ((), ())), preferred...  26.7 us
    dot_general x8, matrix products, tissue(): jnp.dot(dscore, acceptors, preferred_element_type=jnp.float32) * scale  21.4 us
    all_gather x1, waiting for transfers between devices, local(): lax.all_gather(acceptor_local, ('don', 'acc'), axis=0, tiled=True)  20 us
    dynamic_update_slice x16, local copies, waits for them, and re-layouts, local(): summed, counted, dproj = lax.map(tissue, (weights, targets_dev, weighting))  11.8 us
    reduce_sum x8, other arithmetic, tissue(): picked = jnp.sum(jnp.where(is_target, scores, 0.0), axis=1)  11.1 us
    all_gather x1, waiting for transfers between devices, local(): lax.all_gather(dproj, 'don', axis=1, tiled=True)  10.4 us
  transfers between devices with their start and end apart: 2, of which 2 were waited for; matrix products, arithmetic and copies ran while one was open for 3% of the time, Pallas kernels for 0%

commit v1 on v0

v1 whole, which is shorter than its diff:
```python
import functools

import jax
import jax.numpy as jnp
from jax import lax
from jax.experimental import pallas as pl
from jax.experimental.pallas import tpu as pltpu
from jax.sharding import PartitionSpec as P

BF16 = jnp.bfloat16
F32 = jnp.float32


def round_up(n, m):
    return (n + m - 1) // m * m


def row_chunk(n, limit=416):
    best = 16
    for r in range(16, limit + 1, 16):
        if n % r == 0:
            best = r
    return best


def ranks(counts, slots, width):
    shards = counts.shape[0]
    col = lax.broadcasted_iota(jnp.int32, (8, width), 1)

    def step(k, carry):
        first, rank = carry
        within = col - k * slots
        live = (within >= 0) & (within < counts[k])
        return first + counts[k], jnp.where(live, first + within, rank)

    return lax.fori_loop(0, shards, step, (jnp.int32(0), jnp.full((8, width), -1, jnp.int32)))[1]


def labels(counts, slots, width):
    shards = counts.shape[0]
    col = lax.broadcasted_iota(jnp.int32, (8, width), 1)

    def step(k, carry):
        last, label = carry
        last = last + counts[k]
        return last, label + jnp.where(col >= last, slots - counts[k], 0)

    return lax.fori_loop(0, shards, step, (jnp.int32(0), col))[1]


def compute_kernel(
    slots, live, dcnt, acnt, x_ref, comb_ref, w_ref, grad_ref, sums_ref,
    d_s, dt_s, a_s, cols_s, lab_s, out_s, sem,
):
    t = pl.program_id(0)
    tissues = pl.num_programs(0)
    sites, width = x_ref.shape[0], x_ref.shape[1] // 2
    rows, padded = d_s.shape[0], a_s.shape[0]
    parts, _, chunk = dt_s.shape
    depth = out_s.shape[1]
    scale = width ** (-0.5)

    @pl.when(t == 0)
    def _():
        rank_d = ranks(dcnt, slots, sites)[:1]
        rank_a = ranks(acnt, slots, sites)[:1]
        lab_s[...] = labels(acnt, slots, padded)
        comb = comb_ref[...]
        mask = (comb & 1).astype(F32)
        low = ((comb >> 1) & 255).astype(F32)
        high = (comb >> 9).astype(F32)
        table = jnp.concatenate([mask, low, high], axis=0).astype(BF16)
        for c in range(parts):
            row = lax.broadcasted_iota(jnp.int32, (chunk, sites), 0) + c * chunk
            pick = jnp.where(row == rank_d, 1.0, 0.0).astype(BF16)
            d = jnp.dot(pick, x_ref[:, :width], preferred_element_type=F32)
            d_s[c * chunk : (c + 1) * chunk, :] = d.astype(BF16)
            dt_s[c] = jnp.transpose(d).astype(BF16)
            cols_s[c * chunk : (c + 1) * chunk, :] = lax.dot_general(
                pick, table, (((1,), (1,)), ((), ())), preferred_element_type=F32
            )
        step = row_chunk(padded, 512)
        for c in range(padded // step):
            row = lax.broadcasted_iota(jnp.int32, (step, sites), 0) + c * step
            pick = jnp.where(row == rank_a, 1.0, 0.0).astype(BF16)
            a_s[c * step : (c + 1) * step, :] = jnp.dot(
                pick, x_ref[:, width:], preferred_element_type=F32
            ).astype(BF16)
        sums_ref[...] = jnp.zeros_like(sums_ref)

    lane = lax.broadcasted_iota(jnp.int32, (1, padded), 1)
    valid = lane < live
    label = lab_s[:1, :]
    tis = comb_ref.shape[0]
    pick_lane = lax.broadcasted_iota(jnp.int32, (chunk, 3 * tis), 1)
    don = lax.axis_index("don")
    start = pl.multiple_of(don * depth, depth)
    total = jnp.zeros((depth, padded), F32)
    lost = jnp.zeros((), F32)
    count = jnp.zeros((), F32)
    for c in range(parts):
        span = slice(c * chunk, (c + 1) * chunk)
        proj = jnp.dot(d_s[span, :], w_ref[0], preferred_element_type=F32).astype(BF16)
        score = (
            lax.dot_general(proj, a_s[...], (((1,), (1,)), ((), ())), preferred_element_type=F32)
            * scale
        )
        score = jnp.where(valid, score, -1e30)
        cols = cols_s[span, :]
        weight = jnp.sum(jnp.where(pick_lane == t, cols, 0.0), axis=1, keepdims=True)
        low = jnp.sum(jnp.where(pick_lane == t + tis, cols, 0.0), axis=1, keepdims=True)
        high = jnp.sum(jnp.where(pick_lane == t + 2 * tis, cols, 0.0), axis=1, keepdims=True)
        target = (high * 256.0 + low).astype(jnp.int32)
        highest = jnp.max(score, axis=1, keepdims=True)
        expo = jnp.where(valid, jnp.exp(score - highest), 0.0)
        summed = jnp.sum(expo, axis=1, keepdims=True)
        hit = label == target
        picked = jnp.sum(jnp.where(hit, score, 0.0), axis=1, keepdims=True)
        lost = lost + jnp.sum(weight * (highest + jnp.log(summed) - picked))
        count = count + jnp.sum(weight)
        prob = expo * (weight / summed)
        dscore = jnp.where(hit, prob - weight, prob).astype(BF16)
        total = total + jnp.dot(
            dt_s[c, pl.ds(start, depth), :], dscore, preferred_element_type=F32
        )
    total = total * scale
    slot = lax.rem(t, 2)

    def out_copy(which, at):
        return pltpu.make_async_copy(out_s.at[which], grad_ref.at[:, at, :], sem.at[which])

    @pl.when(t >= 2)
    def _():
        out_copy(slot, t - 2).wait()

    out_s[slot] = jnp.dot(total.astype(BF16), a_s[...], preferred_element_type=F32)
    out_copy(slot, t).start()
    first = lax.broadcasted_iota(jnp.int32, sums_ref.shape, 0) == 0
    sums_ref[...] += jnp.where(first, lost, count)

    @pl.when(t == tissues - 1)
    def _():
        out_copy(1 - slot, t - 1).wait()
        out_copy(slot, t).wait()


def compute(slots, donors_all, dcnt, acnt, x, comb, weights, depth):
    tissues, width = weights.shape[0], weights.shape[1]
    sites = x.shape[0]
    shards = acnt.shape[0]
    live = shards * (slots + 1) // 2
    rows = round_up(live, 16)
    padded = round_up(live, 128)
    chunk = row_chunk(rows)
    return pl.pallas_call(
        functools.partial(compute_kernel, slots, live),
        grid=(tissues,),
        in_specs=[
            pl.BlockSpec(memory_space=pltpu.SMEM),
            pl.BlockSpec(memory_space=pltpu.SMEM),
            pl.BlockSpec(memory_space=pltpu.VMEM),
            pl.BlockSpec(memory_space=pltpu.VMEM),
            pl.BlockSpec((1, width, width), lambda t: (t, 0, 0)),
        ],
        out_specs=[
            pl.BlockSpec(memory_space=pl.ANY),
            pl.BlockSpec((8, 128), lambda t: (0, 0)),
        ],
        out_shape=[
            jax.ShapeDtypeStruct((depth, tissues, width), F32),
            jax.ShapeDtypeStruct((8, 128), F32),
        ],
        scratch_shapes=[
            pltpu.VMEM((rows, width), BF16),
            pltpu.VMEM((rows // chunk, width, chunk), BF16),
            pltpu.VMEM((padded, width), BF16),
            pltpu.VMEM((rows, 3 * tissues), F32),
            pltpu.VMEM((8, padded), jnp.int32),
            pltpu.VMEM((2, depth, width), F32),
            pltpu.SemaphoreType.DMA((2,)),
        ],
        compiler_params=pltpu.CompilerParams(vmem_limit_bytes=60 * 1024 * 1024),
    )(dcnt, acnt, x, comb, weights)


def local(
    don_size,
    donor_emb,
    acceptor_emb,
    donor_pos,
    acceptor_pos,
    donor_count,
    acceptor_count,
    target,
    junction_mask,
    weights,
):
    slots = donor_pos.shape[0]
    tis_dev, width = weights.shape[0], weights.shape[1]
    column = lax.axis_index("acc")
    donor_local = donor_emb.at[donor_pos].get(mode="promise_in_bounds")
    acceptor_local = acceptor_emb.at[acceptor_pos].get(mode="promise_in_bounds")
    mine = jnp.concatenate([donor_local, acceptor_local], axis=1)
    x = lax.all_gather(mine, ("don", "acc"), axis=0, tiled=True)
    dcnt = lax.all_gather(donor_count, "don", axis=0, tiled=True)
    comb = lax.dynamic_slice_in_dim(target * 2 + junction_mask, column * tis_dev, tis_dev, 0)
    comb = lax.all_gather(comb, "don", axis=1, tiled=True)
    grad_weight, sums = compute(
        slots, None, dcnt, acceptor_count, x, comb, weights, width // don_size
    )
    sums = lax.psum(sums[:2, 0], "acc")
    return sums[0] / jnp.maximum(sums[1], 1.0), grad_weight


def solution(mesh):
    return jax.shard_map(
        functools.partial(local, mesh.shape["don"]),
        mesh=mesh,
        in_specs=(
            P(("don", "acc"), None),
            P(("don", "acc"), None),
            P(("don", "acc")),
            P(("don", "acc")),
            P("don"),
            P(),
            P(None, "don"),
            P(None, "don"),
            P("acc", None, None),
        ),
        out_specs=(P(), P("don", "acc", None)),
        check_vma=False,
    )
```

time: 242 us -> 128 us (0.53)
  matrix products: 54 us -> 0 us
  blocking collectives: 82.3 us -> 32.2 us
  other arithmetic: 25.9 us -> 2.2 us
  Pallas kernels: 0 us -> 23 us
  local copies, waits for them, and re-layouts: 31 us -> 8.74 us
  waiting for transfers between devices: 30.5 us -> 43.7 us
    dot_general x17 -> x0, matrix products: 54 us -> none  [the longest x8 26.7 us: tissue(): lax.dot_general(projected, acceptors, (((1,), (1,)), ((), ())), preferred...]
    all_gather x1, blocking collectives: 32.6 us -> 6.19 us  [local(): comb = lax.all_gather(comb, 'don', axis=1, tiled=True)]
    pallas_call x0 -> x1, Pallas kernels: none -> 23 us  [compute(): pl.pallas_call(functools.partial(compute_kernel, slots, live), grid=(tiss...]
    reduce_sum x26 -> x0, other arithmetic: 22.7 us -> none  [the longest x8 11.1 us: tissue(): picked = jnp.sum(jnp.where(is_target, scores, 0.0), axis=1)]
    psum x1, blocking collectives: 39.5 us -> 20.2 us  [local(): sums = lax.psum(sums[:2, 0], 'acc')]
    all_gather x2 -> x1, waiting for transfers between devices: 30.4 us -> 43.7 us  [local(): x = lax.all_gather(mine, ('don', 'acc'), axis=0, tiled=True)]
    dynamic_update_slice x16 -> x0, local copies, waits for them, and re-layouts: 11.8 us -> none  [local(): summed, counted, dproj = lax.map(tissue, (weights, targets_dev, weighting))]
    all_to_all x1 -> x0, blocking collectives: 10.2 us -> none  [local(): lax.all_to_all(donors, 'don', split_axis=1, concat_axis=0, tiled=True)]
  transfers between devices with their start and end apart: 2 -> 1, of which waited for: 2 -> 1; matrix products, arithmetic and copies ran while one was open for 3% -> 3% of each run, Pallas kernels for 0% -> 0%
where the time goes in v1:
time: 128 us; the launch traced here: 127 us
  waiting for transfers between devices  43.7 us (34%)
  blocking collectives  32.2 us (25%)
  Pallas kernels  23 us (18%)
  between operations  17.2 us (13%)
  local copies, waits for them, and re-layouts  8.74 us (7%)
  other arithmetic  2.2 us (2%)
    all_gather x1, waiting for transfers between devices, local(): x = lax.all_gather(mine, ('don', 'acc'), axis=0, tiled=True)  43.7 us
    pallas_call x1, Pallas kernels, compute(): pl.pallas_call(functools.partial(compute_kernel, slots, live), grid=(tiss...  23 us
    psum x1, blocking collectives, local(): sums = lax.psum(sums[:2, 0], 'acc')  20.2 us
    all_gather x1, blocking collectives, local(): comb = lax.all_gather(comb, 'don', axis=1, tiled=True)  6.19 us
    unnamed x1, blocking collectives  5.87 us
    unnamed x6, local copies, waits for them, and re-layouts  3.81 us
    gather x1, local copies, waits for them, and re-layouts, local(): acceptor_local = acceptor_emb.at[acceptor_pos].get(mode='promise_in_bounds')  2.92 us
  transfers between devices with their start and end apart: 1, of which 1 were waited for; matrix products, arithmetic and copies ran while one was open for 3% of the time, Pallas kernels for 0%

profile of v1, /device:TPU:0, one launch (start us, length us, event | category | flops | bytes accessed | tf_op | source)
XLA Modules:
  0.0 127.2 jit_solution(12594003310183813639)
XLA Ops:
  7.2 0.0 copy-start
  7.2 0.0 all-gather.3.cloned.1.call-start
  7.2 0.8 compare_select_fusion
  8.1 1.0 copy-done
  9.1 0.6 gather_fusion
  9.7 2.9 %gather_fusion.1 = bf16[24,768]{1,0:T(8,128)(2,1)S(1)} fusion(bf16[2048,768]{1,0:T(8,128)(2,1)} %param.10, s32[1024]{0:T(1024)S(1)} %pad_clamp_fusion), kind=kCustom, calls=%fused_computation.1 | custom fusion | bytes 73824 | tf_op jit(solution)/shard_map/gather | solution.py:202
  12.6 0.6 pad_maximum_fusion
  13.3 0.0 all-gather.3.cloned.1.call-update
  13.3 0.7 fusion
  14.0 6.2 %all-gather = s32[4,192,8]{1,2,0:T(8,128)S(1)} all-gather(s32[1,192,8]{1,2,0:T(8,128)S(1)} %fusion), channel_id=1, replica_groups=mesh['don'=4,'acc'=8] {'don'}, dimensions={0}, use_global_device_ids=true | all-gather | bytes 30720 | tf_op jit(solution)/shard_map/all_gather | solution.py:207
  20.2 0.7 reshape.29
  20.9 1.2 dynamic-slice
  22.8 0.9 dynamic-update-slice
  23.7 5.9 %all-reduce.dcnt = s32[32]{0:T(128)} all-reduce(s32[32]{0:T(128)S(1)} %dynamic-update-slice), channel_id=1, replica_groups=mesh['don'=4,'acc'=8] {'don'}, use_global_device_ids=true, to_apply=%add | all-reduce | flops 32 | bytes 256
  29.5 43.7 %all-gather.3.cloned.1.call-done.x_ref = bf16[768,1536]{1,0:T(8,128)(2,1)} async-done(((bf16[24,1536]{1,0:T(8,128)(2,1)}), bf16[768,1536]{1,0:T(8,128)(2,1)}) %all-gather.3.cloned.1.call-update) | async-done | bytes 2359312 | tf_op jit(solution)/shard_map/all_gather | solution.py:204
  73.3 23.0 %shard_map.104 = (f32[192,8,768]{2,1,0:T(8,128)}, f32[8,128]{1,0:T(8,128)}) custom-call(s32[32]{0:T(128)} %all-reduce.dcnt, s32[32]{0:T(128)} %acnt.1, bf16[768,1536]{1,0:T(8,128)(2,1)} %all-gather.3.cloned.1.call-done.x_ref, s32[8,768]{1,0:T(8,128)} %bitcast.9, bf16[8,768,768]{2,1,0:T(8,128)(2,1)} %w_ref.1), custom_call_target="tpu_custom_call" | custom-call | tf_op jit(solution)/shard_map/pallas_call | solution.py:155
  96.3 0.8 slice_reduce_fusion
  97.1 20.2 %psum.7 = f32[2]{0:T(128)S(1)} all-reduce(f32[2]{0:T(128)S(1)} %slice_reduce_fusion), channel_id=1, replica_groups=mesh['don'=4,'acc'=8] {'acc'}, use_global_device_ids=true, to_apply=%region_0.0 | all-reduce | flops 2 | bytes 16 | tf_op jit(solution)/shard_map/psum | solution.py:211
  117.2 0.6 fusion.1
  (4 shorter events, 0.0 us)
Async XLA Ops:
  7.2 1.9 %copy-start = (bf16[2048,768]{1,0:T(8,128)(2,1)S(1)}, bf16[2048,768]{1,0:T(8,128)(2,1)}, u32[]{:S(2)}) copy-start(bf16[2048,768]{1,0:T(8,128)(2,1)} %param.9) | copy-start | bytes 9437188
  7.2 66.1 %all-gather.3.cloned.1.call-start = ((), (), s32[]{:S(2)}) async-start(), calls=%async_computation | async-start | bytes 2433024 | tf_op jit(solution)/shard_map/all_gather | solution.py:204
Sparse Core Ops, SparseCore 0:
  13.4 59.7 all-gather.2

commit v2 on v1

--- a/solution.py
+++ b/solution.py
@@ -144,7 +144,7 @@
         out_copy(slot, t).wait()
 
 
-def compute(slots, donors_all, dcnt, acnt, x, comb, weights, depth):
+def compute(slots, dcnt, acnt, x, comb, weights, depth):
     tissues, width = weights.shape[0], weights.shape[1]
     sites = x.shape[0]
     shards = acnt.shape[0]
@@ -183,8 +183,205 @@
     )(dcnt, acnt, x, comb, weights)
 
 
+MESH = pl.DeviceIdType.MESH
+
+
+def gather_kernel(don_size, acc_size, inner, x_ref, comb_ref, cnt_ref, xs_ref, combs_ref, cnts_ref,
+                  send_sem, recv_sem, side_send, side_recv, own_sem):
+    outer = acc_size // inner
+    chips = don_size // 2
+    alternate = chips == inner
+    don, acc = lax.axis_index("don"), lax.axis_index("acc")
+    core, x = lax.rem(don, 2), don // 2
+    o, i = acc // inner, lax.rem(acc, inner)
+    if alternate:
+        b = core * x + (1 - core) * i
+        c = core * i + (1 - core) * x
+        b_size, c_size = inner, inner
+    else:
+        b, c, b_size, c_size = i, x, inner, chips
+
+    def place(which, oo, bb, cc):
+        if alternate:
+            xx = core * bb + (1 - core) * cc
+            ii = core * cc + (1 - core) * bb
+        else:
+            xx, ii = cc, bb
+        return (xx * 2 + which, oo * inner + ii)
+
+    def away(at, k, size):
+        return lax.rem(at + k, size)
+
+    peers = [place(core, away(o, k, outer), b, c) for k in range(1, outer)]
+    peers += [place(core, o, away(b, k, b_size), c) for k in range(1, b_size)]
+    peers += [place(core, o, b, away(c, k, c_size)) for k in range(1, c_size)]
+    peers += [place(1 - core, o, b, c)]
+    others = [(lax.rem(don + k, don_size), acc) for k in range(1, don_size)]
+    barrier = pltpu.get_barrier_semaphore()
+    for peer in peers + others:
+        pl.semaphore_signal(barrier, inc=1, device_id=peer, device_id_type=MESH)
+    pl.semaphore_wait(barrier, len(peers) + len(others))
+
+    sent = []
+    held = don * acc_size + acc
+
+    def send(source, slot, peer):
+        copy = pltpu.make_async_remote_copy(
+            src_ref=source,
+            dst_ref=xs_ref.at[slot],
+            send_sem=send_sem.at[len(sent)],
+            recv_sem=recv_sem.at[slot],
+            device_id=peer,
+            device_id_type=MESH,
+        )
+        copy.start()
+        sent.append(copy)
+
+    def slot_of(at):
+        return at[0] * acc_size + at[1]
+
+    def arrived(slot):
+        pltpu.make_async_copy(x_ref, xs_ref.at[slot], recv_sem.at[slot]).wait()
+
+    def forward(source, slot, hops):
+        if hops >= 3:
+            for k in range(1, outer):
+                send(source, slot, place(core, away(o, k, outer), b, c))
+        if hops >= 2:
+            for k in range(1, b_size):
+                send(source, slot, place(core, o, away(b, k, b_size), c))
+        if hops >= 1:
+            for k in range(1, c_size):
+                send(source, slot, place(core, o, b, away(c, k, c_size)))
+        send(source, slot, place(1 - core, o, b, c))
+
+    forward(x_ref, held, 3)
+    side = []
+    for k, peer in enumerate(others):
+        for j, (source, target) in enumerate(((comb_ref, combs_ref), (cnt_ref, cnts_ref))):
+            copy = pltpu.make_async_remote_copy(
+                src_ref=source,
+                dst_ref=target.at[don],
+                send_sem=side_send.at[k, j],
+                recv_sem=side_recv.at[k, j],
+                device_id=peer,
+                device_id_type=MESH,
+            )
+            copy.start()
+            side.append(copy)
+    own = [
+        pltpu.make_async_copy(x_ref, xs_ref.at[held], own_sem.at[0]),
+        pltpu.make_async_copy(comb_ref, combs_ref.at[don], own_sem.at[1]),
+        pltpu.make_async_copy(cnt_ref, cnts_ref.at[don], own_sem.at[2]),
+    ]
+    for copy in own:
+        copy.start()
+
+    def relay(slot, hops):
+        arrived(slot)
+        forward(xs_ref.at[slot], slot, hops)
+
+    for ko in range(outer):
+        oo = away(o, ko, outer)
+        if ko:
+            relay(slot_of(place(core, oo, b, c)), 2)
+        for kb in range(1, b_size):
+            relay(slot_of(place(core, oo, away(b, kb, b_size), c)), 1)
+    for ko in range(outer):
+        for kb in range(b_size):
+            for kc in range(1, c_size):
+                relay(slot_of(place(core, away(o, ko, outer), away(b, kb, b_size), away(c, kc, c_size))), 0)
+    for ko in range(outer):
+        for kx in range(chips):
+            for ki in range(inner):
+                at = (away(x, kx, chips) * 2 + 1 - core, away(o, ko, outer) * inner + away(i, ki, inner))
+                arrived(slot_of(at))
+    for copy in sent:
+        copy.wait_send()
+    for copy in side:
+        copy.wait()
+    for copy in own:
+        copy.wait()
+
+
+def gather(don_size, acc_size, x, comb, counts):
+    inner = 1
+    while (2 * inner) ** 2 <= acc_size:
+        inner *= 2
+    outer, chips = acc_size // inner, don_size // 2
+    half = don_size * acc_size // 2
+    per_core = (outer - 1) + outer * (inner - 1) + outer * inner * (chips - 1)
+    any_space = pl.BlockSpec(memory_space=pl.ANY)
+    shards = don_size * acc_size
+    return pl.pallas_call(
+        functools.partial(gather_kernel, don_size, acc_size, inner),
+        in_specs=[any_space] * 3,
+        out_specs=[any_space] * 3,
+        out_shape=[
+            jax.ShapeDtypeStruct((shards,) + x.shape, x.dtype),
+            jax.ShapeDtypeStruct((don_size,) + comb.shape, comb.dtype),
+            jax.ShapeDtypeStruct((don_size,) + counts.shape, counts.dtype),
+        ],
+        scratch_shapes=[
+            pltpu.SemaphoreType.DMA((per_core + half,)),
+            pltpu.SemaphoreType.DMA((shards,)),
+            pltpu.SemaphoreType.DMA((don_size - 1, 2)),
+            pltpu.SemaphoreType.DMA((don_size - 1, 2)),
+            pltpu.SemaphoreType.DMA((3,)),
+        ],
+        compiler_params=pltpu.CompilerParams(collective_id=0, has_side_effects=True),
+    )(x, comb, counts)
+
+
+def loss_kernel(acc_size, sums_ref, loss_ref, land, send_sem, recv_sem, own_sem):
+    don, acc = lax.axis_index("don"), lax.axis_index("acc")
+    peers = [(don, lax.rem(acc + k, acc_size)) for k in range(1, acc_size)]
+    barrier = pltpu.get_barrier_semaphore()
+    for peer in peers:
+        pl.semaphore_signal(barrier, inc=1, device_id=peer, device_id_type=MESH)
+    pl.semaphore_wait(barrier, acc_size - 1)
+    copies = []
+    for k, peer in enumerate(peers):
+        copy = pltpu.make_async_remote_copy(
+            src_ref=sums_ref,
+            dst_ref=land.at[acc],
+            send_sem=send_sem.at[k],
+            recv_sem=recv_sem.at[k],
+            device_id=peer,
+            device_id_type=MESH,
+        )
+        copy.start()
+        copies.append(copy)
+    own = pltpu.make_async_copy(sums_ref, land.at[acc], own_sem)
+    own.start()
+    own.wait()
+    for copy in copies:
+        copy.wait()
+    total = land[0]
+    for k in range(1, acc_size):
+        total = total + land[k]
+    loss_ref[...] = jnp.broadcast_to(total[:1] / jnp.maximum(total[1:2], 1.0), loss_ref.shape)
+
+
+def loss_sum(acc_size, sums):
+    return pl.pallas_call(
+        functools.partial(loss_kernel, acc_size),
+        in_specs=[pl.BlockSpec(memory_space=pltpu.VMEM)],
+        out_specs=pl.BlockSpec(memory_space=pltpu.VMEM),
+        out_shape=jax.ShapeDtypeStruct(sums.shape, F32),
+        scratch_shapes=[
+            pltpu.VMEM((acc_size,) + sums.shape, F32),
+            pltpu.SemaphoreType.DMA((acc_size - 1,)),
+            pltpu.SemaphoreType.DMA((acc_size - 1,)),
+            pltpu.SemaphoreType.DMA,
+        ],
+        compiler_params=pltpu.CompilerParams(collective_id=1, has_side_effects=True),
+    )(sums)
+
+
 def local(
     don_size,
+    acc_size,
     donor_emb,
     acceptor_emb,
     donor_pos,
@@ -201,20 +398,19 @@
     donor_local = donor_emb.at[donor_pos].get(mode="promise_in_bounds")
     acceptor_local = acceptor_emb.at[acceptor_pos].get(mode="promise_in_bounds")
     mine = jnp.concatenate([donor_local, acceptor_local], axis=1)
-    x = lax.all_gather(mine, ("don", "acc"), axis=0, tiled=True)
-    dcnt = lax.all_gather(donor_count, "don", axis=0, tiled=True)
     comb = lax.dynamic_slice_in_dim(target * 2 + junction_mask, column * tis_dev, tis_dev, 0)
-    comb = lax.all_gather(comb, "don", axis=1, tiled=True)
+    x, comb, dcnt = gather(don_size, acc_size, mine, comb, donor_count[None, :])
+    x = x.reshape(-1, 2 * width)
+    comb = jnp.transpose(comb, (1, 0, 2)).reshape(tis_dev, -1)
     grad_weight, sums = compute(
-        slots, None, dcnt, acceptor_count, x, comb, weights, width // don_size
+        slots, dcnt.reshape(-1), acceptor_count, x, comb, weights, width // don_size
     )
-    sums = lax.psum(sums[:2, 0], "acc")
-    return sums[0] / jnp.maximum(sums[1], 1.0), grad_weight
+    return loss_sum(acc_size, sums)[0, 0], grad_weight
 
 
 def solution(mesh):
     return jax.shard_map(
-        functools.partial(local, mesh.shape["don"]),
+        functools.partial(local, mesh.shape["don"], mesh.shape["acc"]),
         mesh=mesh,
         in_specs=(
             P(("don", "acc"), None),

time: 128 us -> 73.8 us (0.58)
  waiting for transfers between devices: 43.7 us -> 0 us
  Pallas kernels: 23 us -> 61.2 us
  blocking collectives: 32.2 us -> 0 us
  between operations: 17.2 us -> 0.68 us
  other arithmetic: 2.2 us -> 4.25 us
  local copies, waits for them, and re-layouts: 8.74 us -> 7.29 us
    all_gather x1 -> x0, waiting for transfers between devices: 43.7 us -> none  [local(): x = lax.all_gather(mine, ('don', 'acc'), axis=0, tiled=True)]
    pallas_call x0 -> x2, Pallas kernels: none -> 38.2 us  [the longest x1 29.1 us: gather(): pl.pallas_call(functools.partial(gather_kernel, don_size, acc_size, inner...]
    psum x1 -> x0, blocking collectives: 20.2 us -> none  [local(): sums = lax.psum(sums[:2, 0], 'acc')]
    all_gather x1 -> x0, blocking collectives: 6.19 us -> none  [local(): comb = lax.all_gather(comb, 'don', axis=1, tiled=True)]
    unnamed x1 -> x0, blocking collectives: 5.87 us -> none
    unnamed x6 -> x2, local copies, waits for them, and re-layouts: 3.81 us -> 0.01 us
    add x0 -> x1, other arithmetic: none -> 1.42 us  [local(): target * 2 + junction_mask]
    pallas_call x0 -> x1, other arithmetic: none -> 1.35 us  [gather(): pl.pallas_call(functools.partial(gather_kernel, don_size, acc_size, inner...]
  transfers between devices with their start and end apart: 1 -> 0, of which waited for: 1 -> 0; matrix products, arithmetic and copies ran while one was open for 3% -> 0% of each run, Pallas kernels for 0% -> 0%
where the time goes in v2:
time: 73.8 us; the launch traced here: 73.4 us
  Pallas kernels  61.2 us (83%)
  local copies, waits for them, and re-layouts  7.29 us (10%)
  other arithmetic  4.25 us (6%)
    pallas_call x1, Pallas kernels, gather(): pl.pallas_call(functools.partial(gather_kernel, don_size, acc_size, inner...  29.1 us
    pallas_call x1, Pallas kernels, compute(): pl.pallas_call(functools.partial(compute_kernel, slots, live), grid=(tiss...  23 us
    pallas_call x1, Pallas kernels, loss_sum(): pl.pallas_call(functools.partial(loss_kernel, acc_size), in_specs=[pl.Blo...  9.08 us
    gather x1, local copies, waits for them, and re-layouts, local(): acceptor_local = acceptor_emb.at[acceptor_pos].get(mode='promise_in_bounds')  2.92 us

profile of v2, /device:TPU:0, one launch (start us, length us, event | category | flops | bytes accessed | tf_op | source)
XLA Modules:
  0.0 73.4 jit_solution(5028482046302100633)
XLA Ops:
  0.6 0.0 copy-start
  0.6 0.8 %compare_select_fusion = (s32[24]{0:T(128)S(1)}, s32[24]{0:T(128)S(1)}) fusion(s32[24]{0:T(128)} %param.12, s32[24]{0:T(128)} %param.11), kind=kLoop, calls=%fused_computation.7 | loop fusion | flops 144 | bytes 384 | tf_op jit(solution)/shard_map/select_n | solution.py:399
  1.5 1.4 %dynamic-slice_add_fusion.comb_ref = s32[8,192]{1,0:T(8,128)} fusion(s32[64,192]{1,0:T(8,128)} %param.16, s32[]{:T(128)S(6)} %select_n.11, s32[64,192]{1,0:T(8,128)} %param.15), kind=kLoop, calls=%fused_computation.3 | loop fusion | flops 3072 | bytes 18436 | tf_op jit(solution)/shard_map/add | solution.py:401
  2.9 0.0 copy-done
  2.9 0.6 gather_fusion
  3.5 2.9 %gather_fusion.1 = bf16[24,768]{1,0:T(8,128)(2,1)S(1)} fusion(bf16[2048,768]{1,0:T(8,128)(2,1)} %param.10, s32[1024]{0:T(1024)S(1)} %pad_clamp_fusion), kind=kCustom, calls=%fused_computation.1 | custom fusion | bytes 73824 | tf_op jit(solution)/shard_map/gather | solution.py:399
  6.5 0.6 pad_maximum_fusion.x_ref
  7.1 29.1 %shard_map.104 = (bf16[32,24,1536]{2,1,0:T(8,128)(2,1)}, s32[4,8,192]{2,1,0:T(8,128)}, s32[4,1,8]{2,1,0:T(1,128)}) custom-call(bf16[24,1536]{1,0:T(8,128)(2,1)} %pad_maximum_fusion.x_ref, s32[8,192]{1,0:T(8,128)} %dynamic-slice_add_fusion.comb_ref, s32[1,8]{1,0:T(1,128)} %bitcast.6), custom_call_target="tpu_custom_call" | custom-call | tf_op jit(solution)/shard_map/pallas_call | solution.py:316
  36.2 0.5 broadcast.23
  36.7 1.3 %reduce.3 = s32[4,8]{1,0:T(4,128)S(1)} reduce(s32[4,1,8]{2,1,0:T(1,128)} %get-tuple-element.7, s32[]{:T(128)} %broadcast.23), dimensions={1}, to_apply=%get-tuple-element.7.reduce_sub_computation.3 | reduce | bytes 260 | tf_op jit(solution)/shard_map/pallas_call | solution.py:316
  38.0 0.6 reshape.13.dcnt
  38.6 0.8 %copy.11 = s32[8,4,192]{2,1,0:T(4,128)S(1)} copy(s32[8,4,192]{2,0,1:T(8,128)} %bitcast.5) | data formatting | bytes 49152 | tf_op jit(solution)/shard_map/transpose | solution.py:404
  39.4 0.7 reshape.15.comb_ref
  40.1 23.0 %shard_map.105 = (f32[192,8,768]{2,1,0:T(8,128)}, f32[8,128]{1,0:T(8,128)}) custom-call(s32[32]{0:T(128)} %reshape.13.dcnt, s32[32]{0:T(128)} %acnt.1, bf16[768,1536]{1,0:T(8,128)(2,1)} %bitcast.4, s32[8,768]{1,0:T(8,128)} %reshape.15.comb_ref, bf16[8,768,768]{2,1,0:T(8,128)(2,1)} %w_ref.1), custom_call_target="tpu_custom_call" | custom-call | tf_op jit(solution)/shard_map/pallas_call | solution.py:155
  63.1 9.1 %shard_map.106 = f32[8,128]{1,0:T(8,128)} custom-call(f32[8,128]{1,0:T(8,128)} %get-tuple-element.10.sums_ref), custom_call_target="tpu_custom_call" | custom-call | tf_op jit(solution)/shard_map/pallas_call | solution.py:367
  72.2 1.2 %slice.3 = f32[1,1]{1,0:T(1,128)} slice(f32[8,128]{1,0:T(8,128)} %shard_map.106), slice={[0:1], [0:1]} | slice | bytes 8 | tf_op jit(solution)/shard_map/slice | solution.py:408
  (2 shorter events, 0.0 us)
Async XLA Ops:
  0.6 2.3 %copy-start = (bf16[2048,768]{1,0:T(8,128)(2,1)S(1)}, bf16[2048,768]{1,0:T(8,128)(2,1)}, u32[]{:S(2)}) copy-start(bf16[2048,768]{1,0:T(8,128)(2,1)} %param.9) | copy-start | bytes 9437188

commit v3 on v2

--- a/solution.py
+++ b/solution.py
@@ -24,33 +24,35 @@
 
 
 def ranks(counts, slots, width):
-    shards = counts.shape[0]
+    groups, _, each = counts.shape
+    shards = groups * each
     col = lax.broadcasted_iota(jnp.int32, (8, width), 1)
 
     def step(k, carry):
         first, rank = carry
+        number = counts[k // each, 0, lax.rem(k, each)]
         within = col - k * slots
-        live = (within >= 0) & (within < counts[k])
-        return first + counts[k], jnp.where(live, first + within, rank)
+        live = (within >= 0) & (within < number)
+        return first + number, jnp.where(live, first + within, rank)
 
     return lax.fori_loop(0, shards, step, (jnp.int32(0), jnp.full((8, width), -1, jnp.int32)))[1]
 
 
 def labels(counts, slots, width):
-    shards = counts.shape[0]
+    shards = counts.shape[2]
     col = lax.broadcasted_iota(jnp.int32, (8, width), 1)
 
     def step(k, carry):
         last, label = carry
-        last = last + counts[k]
-        return last, label + jnp.where(col >= last, slots - counts[k], 0)
+        last = last + counts[0, 0, k]
+        return last, label + jnp.where(col >= last, slots - counts[0, 0, k], 0)
 
     return lax.fori_loop(0, shards, step, (jnp.int32(0), col))[1]
 
 
 def compute_kernel(
     slots, live, dcnt, acnt, x_ref, comb_ref, w_ref, grad_ref, sums_ref,
-    d_s, dt_s, a_s, cols_s, lab_s, out_s, sem,
+    d_s, dt_s, a_s, cols_s, lab_s, lost_s, out_s, sem,
 ):
     t = pl.program_id(0)
     tissues = pl.num_programs(0)
@@ -65,20 +67,23 @@
         rank_d = ranks(dcnt, slots, sites)[:1]
         rank_a = ranks(acnt, slots, sites)[:1]
         lab_s[...] = labels(acnt, slots, padded)
-        comb = comb_ref[...]
+        comb = jnp.concatenate([comb_ref[p] for p in range(comb_ref.shape[0])], axis=1)
         mask = (comb & 1).astype(F32)
         low = ((comb >> 1) & 255).astype(F32)
         high = (comb >> 9).astype(F32)
-        table = jnp.concatenate([mask, low, high], axis=0).astype(BF16)
+        table = jnp.concatenate([mask, low], axis=0).astype(BF16)
+        upper = jnp.concatenate([jnp.zeros_like(high), high], axis=0).astype(BF16)
         for c in range(parts):
             row = lax.broadcasted_iota(jnp.int32, (chunk, sites), 0) + c * chunk
             pick = jnp.where(row == rank_d, 1.0, 0.0).astype(BF16)
             d = jnp.dot(pick, x_ref[:, :width], preferred_element_type=F32)
             d_s[c * chunk : (c + 1) * chunk, :] = d.astype(BF16)
             dt_s[c] = jnp.transpose(d).astype(BF16)
-            cols_s[c * chunk : (c + 1) * chunk, :] = lax.dot_general(
-                pick, table, (((1,), (1,)), ((), ())), preferred_element_type=F32
-            )
+            low_cols, high_cols = [
+                lax.dot_general(pick, part, (((1,), (1,)), ((), ())), preferred_element_type=F32)
+                for part in (table, upper)
+            ]
+            cols_s[c * chunk : (c + 1) * chunk, :] = low_cols + 256.0 * high_cols
         step = row_chunk(padded, 512)
         for c in range(padded // step):
             row = lax.broadcasted_iota(jnp.int32, (step, sites), 0) + c * step
@@ -86,18 +91,16 @@
             a_s[c * step : (c + 1) * step, :] = jnp.dot(
                 pick, x_ref[:, width:], preferred_element_type=F32
             ).astype(BF16)
-        sums_ref[...] = jnp.zeros_like(sums_ref)
+        lost_s[...] = jnp.zeros_like(lost_s)
 
     lane = lax.broadcasted_iota(jnp.int32, (1, padded), 1)
     valid = lane < live
     label = lab_s[:1, :]
-    tis = comb_ref.shape[0]
-    pick_lane = lax.broadcasted_iota(jnp.int32, (chunk, 3 * tis), 1)
+    tis = comb_ref.shape[1]
+    pick_lane = lax.broadcasted_iota(jnp.int32, (chunk, 2 * tis), 1)
     don = lax.axis_index("don")
     start = pl.multiple_of(don * depth, depth)
     total = jnp.zeros((depth, padded), F32)
-    lost = jnp.zeros((), F32)
-    count = jnp.zeros((), F32)
     for c in range(parts):
         span = slice(c * chunk, (c + 1) * chunk)
         proj = jnp.dot(d_s[span, :], w_ref[0], preferred_element_type=F32).astype(BF16)
@@ -108,16 +111,15 @@
         score = jnp.where(valid, score, -1e30)
         cols = cols_s[span, :]
         weight = jnp.sum(jnp.where(pick_lane == t, cols, 0.0), axis=1, keepdims=True)
-        low = jnp.sum(jnp.where(pick_lane == t + tis, cols, 0.0), axis=1, keepdims=True)
-        high = jnp.sum(jnp.where(pick_lane == t + 2 * tis, cols, 0.0), axis=1, keepdims=True)
-        target = (high * 256.0 + low).astype(jnp.int32)
+        target = jnp.sum(jnp.where(pick_lane == t + tis, cols, 0.0), axis=1, keepdims=True)
+        target = target.astype(jnp.int32)
         highest = jnp.max(score, axis=1, keepdims=True)
         expo = jnp.where(valid, jnp.exp(score - highest), 0.0)
         summed = jnp.sum(expo, axis=1, keepdims=True)
         hit = label == target
         picked = jnp.sum(jnp.where(hit, score, 0.0), axis=1, keepdims=True)
-        lost = lost + jnp.sum(weight * (highest + jnp.log(summed) - picked))
-        count = count + jnp.sum(weight)
+        lost_s[0] += weight * (highest + jnp.log(summed) - picked)
+        lost_s[1] += weight
         prob = expo * (weight / summed)
         dscore = jnp.where(hit, prob - weight, prob).astype(BF16)
         total = total + jnp.dot(
@@ -135,11 +137,11 @@
 
     out_s[slot] = jnp.dot(total.astype(BF16), a_s[...], preferred_element_type=F32)
     out_copy(slot, t).start()
-    first = lax.broadcasted_iota(jnp.int32, sums_ref.shape, 0) == 0
-    sums_ref[...] += jnp.where(first, lost, count)
 
     @pl.when(t == tissues - 1)
     def _():
+        first = lax.broadcasted_iota(jnp.int32, sums_ref.shape, 0) == 0
+        sums_ref[...] = jnp.where(first, jnp.sum(lost_s[0]), jnp.sum(lost_s[1]))
         out_copy(1 - slot, t - 1).wait()
         out_copy(slot, t).wait()
 
@@ -147,7 +149,7 @@
 def compute(slots, dcnt, acnt, x, comb, weights, depth):
     tissues, width = weights.shape[0], weights.shape[1]
     sites = x.shape[0]
-    shards = acnt.shape[0]
+    shards = acnt.shape[2]
     live = shards * (slots + 1) // 2
     rows = round_up(live, 16)
     padded = round_up(live, 128)
@@ -174,13 +176,71 @@
             pltpu.VMEM((rows, width), BF16),
             pltpu.VMEM((rows // chunk, width, chunk), BF16),
             pltpu.VMEM((padded, width), BF16),
-            pltpu.VMEM((rows, 3 * tissues), F32),
+            pltpu.VMEM((rows, 2 * tissues), F32),
             pltpu.VMEM((8, padded), jnp.int32),
+            pltpu.VMEM((2, chunk, 1), F32),
             pltpu.VMEM((2, depth, width), F32),
             pltpu.SemaphoreType.DMA((2,)),
         ],
         compiler_params=pltpu.CompilerParams(vmem_limit_bytes=60 * 1024 * 1024),
     )(dcnt, acnt, x, comb, weights)
+
+
+GROUP = 16
+
+
+def fetch_kernel(
+    dpos, apos, demb_ref, aemb_ref, target_ref, mask_ref, x_ref, comb_ref, dbuf, abuf, sem
+):
+    slots, width = x_ref.shape[0], x_ref.shape[1] // 2
+    sides = ((dpos, demb_ref, dbuf, 0), (apos, aemb_ref, abuf, 1))
+    for pos, emb, buf, which in sides:
+        for k in range(slots):
+            first = pl.multiple_of(pos[k] // GROUP * GROUP, GROUP)
+            pltpu.make_async_copy(
+                emb.at[pl.ds(first, GROUP), :],
+                buf.at[pl.ds(k * GROUP, GROUP), :],
+                sem.at[which],
+            ).start()
+    tis = comb_ref.shape[0]
+    acc = lax.axis_index("acc")
+    comb = target_ref[...] * 2 + mask_ref[...]
+    mine = comb[:tis]
+    for k in range(1, comb.shape[0] // tis):
+        mine = jnp.where(acc == k, comb[k * tis : (k + 1) * tis], mine)
+    comb_ref[...] = mine
+    row = lax.broadcasted_iota(jnp.int32, (slots, slots * GROUP), 0)
+    lane = lax.broadcasted_iota(jnp.int32, (slots, slots * GROUP), 1)
+    for pos, emb, buf, which in sides:
+        want = jnp.zeros((slots, slots * GROUP), jnp.int32)
+        for k in range(slots):
+            want = jnp.where(row == k, k * GROUP + lax.rem(pos[k], GROUP), want)
+        pick = jnp.where(lane == want, 1.0, 0.0).astype(BF16)
+        pltpu.make_async_copy(emb.at[pl.ds(0, slots * GROUP), :], buf, sem.at[which]).wait()
+        x_ref[:, which * width : (which + 1) * width] = jnp.dot(
+            pick, buf[...], preferred_element_type=F32
+        ).astype(BF16)
+
+
+def fetch(dpos, apos, demb, aemb, target, mask, tissues):
+    slots, width = dpos.shape[0], demb.shape[1]
+    smem = pl.BlockSpec(memory_space=pltpu.SMEM)
+    hbm = pl.BlockSpec(memory_space=pl.ANY)
+    vmem = pl.BlockSpec(memory_space=pltpu.VMEM)
+    return pl.pallas_call(
+        fetch_kernel,
+        in_specs=[smem, smem, hbm, hbm, vmem, vmem],
+        out_specs=[vmem, vmem],
+        out_shape=[
+            jax.ShapeDtypeStruct((slots, 2 * width), BF16),
+            jax.ShapeDtypeStruct((tissues, target.shape[1]), jnp.int32),
+        ],
+        scratch_shapes=[
+            pltpu.VMEM((slots * GROUP, width), BF16),
+            pltpu.VMEM((slots * GROUP, width), BF16),
+            pltpu.SemaphoreType.DMA((2,)),
+        ],
+    )(dpos, apos, demb, aemb, target, mask)
 
 
 MESH = pl.DeviceIdType.MESH
@@ -394,16 +454,11 @@
 ):
     slots = donor_pos.shape[0]
     tis_dev, width = weights.shape[0], weights.shape[1]
-    column = lax.axis_index("acc")
-    donor_local = donor_emb.at[donor_pos].get(mode="promise_in_bounds")
-    acceptor_local = acceptor_emb.at[acceptor_pos].get(mode="promise_in_bounds")
-    mine = jnp.concatenate([donor_local, acceptor_local], axis=1)
-    comb = lax.dynamic_slice_in_dim(target * 2 + junction_mask, column * tis_dev, tis_dev, 0)
+    mine, comb = fetch(donor_pos, acceptor_pos, donor_emb, acceptor_emb, target, junction_mask, tis_dev)
     x, comb, dcnt = gather(don_size, acc_size, mine, comb, donor_count[None, :])
     x = x.reshape(-1, 2 * width)
-    comb = jnp.transpose(comb, (1, 0, 2)).reshape(tis_dev, -1)
     grad_weight, sums = compute(
-        slots, dcnt.reshape(-1), acceptor_count, x, comb, weights, width // don_size
+        slots, dcnt, acceptor_count[None, None, :], x, comb, weights, width // don_size
     )
     return loss_sum(acc_size, sums)[0, 0], grad_weight
 

time: 73.8 us -> 67.2 us (0.911)
  local copies, waits for them, and re-layouts: 7.29 us -> 1.19 us
  other arithmetic: 4.25 us -> 0 us
  Pallas kernels: 61.2 us -> 65 us
    gather x2 -> x0, local copies, waits for them, and re-layouts: 3.53 us -> none  [the longest x1 2.92 us: local(): acceptor_local = acceptor_emb.at[acceptor_pos].get(mode='promise_in_bounds')]
    pallas_call x0 -> x1, Pallas kernels: none -> 3.05 us  [fetch(): pl.pallas_call(fetch_kernel, in_specs=[smem, smem, hbm, hbm, vmem, vmem],...]
    add x1 -> x0, other arithmetic: 1.42 us -> none  [local(): target * 2 + junction_mask]
    pallas_call x1 -> x0, other arithmetic: 1.35 us -> none  [gather(): pl.pallas_call(functools.partial(gather_kernel, don_size, acc_size, inner...]
    reshape x2 -> x0, local copies, waits for them, and re-layouts: 1.28 us -> none  [the longest x1 0.68 us: local(): comb = jnp.transpose(comb, (1, 0, 2)).reshape(tis_dev, -1)]
    select_n x1 -> x0, other arithmetic: 0.83 us -> none  [local(): acceptor_local = acceptor_emb.at[acceptor_pos].get(mode='promise_in_bounds')]
    transpose x1 -> x0, local copies, waits for them, and re-layouts: 0.77 us -> none  [local(): comb = jnp.transpose(comb, (1, 0, 2)).reshape(tis_dev, -1)]
where the time goes in v3:
time: 67.2 us; the launch traced here: 66.9 us
  Pallas kernels  65 us (97%)
  local copies, waits for them, and re-layouts  1.19 us (2%)
    pallas_call x1, Pallas kernels, gather(): pl.pallas_call(functools.partial(gather_kernel, don_size, acc_size, inner...  29 us
    pallas_call x1, Pallas kernels, compute(): pl.pallas_call(functools.partial(compute_kernel, slots, live), grid=(tiss...  23.6 us
    pallas_call x1, Pallas kernels, loss_sum(): pl.pallas_call(functools.partial(loss_kernel, acc_size), in_specs=[pl.Blo...  9.41 us
    pallas_call x1, Pallas kernels, fetch(): pl.pallas_call(fetch_kernel, in_specs=[smem, smem, hbm, hbm, vmem, vmem],...  3.05 us

profile of v3, /device:TPU:0, one launch (start us, length us, event | category | flops | bytes accessed | tf_op | source)
XLA Modules:
  0.0 66.9 jit_solution(16689077177240374392)
XLA Ops:
  0.6 3.1 %shard_map.104 = (bf16[24,1536]{1,0:T(8,128)(2,1)}, s32[8,192]{1,0:T(8,128)}) custom-call(s32[24]{0:T(128)} %dpos.1, s32[24]{0:T(128)} %apos.1, bf16[2048,768]{1,0:T(8,128)(2,1)} %demb_ref.1, bf16[2048,768]{1,0:T(8,128)(2,1)} %aemb_ref.1, s32[64,192]{1,0:T(8,128)} %target_ref.1, s32[64,192]{1,0:T(8,128)} %mask_ref.1), custom_call_target="tpu_custom_call" | custom-call | tf_op jit(solution)/shard_map/pallas_call | solution.py:230
  3.7 29.0 %shard_map.105 = (bf16[32,24,1536]{2,1,0:T(8,128)(2,1)}, s32[4,8,192]{2,1,0:T(8,128)}, s32[4,1,8]{2,1,0:T(1,128)}) custom-call(bf16[24,1536]{1,0:T(8,128)(2,1)} %get-tuple-element.9.x_ref, s32[8,192]{1,0:T(8,128)} %get-tuple-element.10.comb_ref, s32[1,8]{1,0:T(1,128)} %bitcast.5), custom_call_target="tpu_custom_call" | custom-call | tf_op jit(solution)/shard_map/pallas_call | solution.py:376
  32.7 23.6 %shard_map.106 = (f32[192,8,768]{2,1,0:T(8,128)}, f32[8,128]{1,0:T(8,128)}) custom-call(s32[4,1,8]{2,1,0:T(1,128)} %get-tuple-element.11.dcnt, s32[1,1,32]{2,1,0:T(1,128)} %bitcast.6, bf16[768,1536]{1,0:T(8,128)(2,1)} %bitcast.4, s32[4,8,192]{2,1,0:T(8,128)} %get-tuple-element.13.comb_ref, bf16[8,768,768]{2,1,0:T(8,128)(2,1)} %w_ref.1), custom_call_target="tpu_custom_call" | custom-call | tf_op jit(solution)/shard_map/pallas_call | solution.py:157
  56.3 9.4 %shard_map.107 = f32[8,128]{1,0:T(8,128)} custom-call(f32[8,128]{1,0:T(8,128)} %get-tuple-element.14.sums_ref), custom_call_target="tpu_custom_call" | custom-call | tf_op jit(solution)/shard_map/pallas_call | solution.py:427
  65.7 1.2 %slice.3 = f32[1,1]{1,0:T(1,128)} slice(f32[8,128]{1,0:T(8,128)} %shard_map.107), slice={[0:1], [0:1]} | slice | bytes 8 | tf_op jit(solution)/shard_map/slice | solution.py:463

commit v4 on v3

--- a/solution.py
+++ b/solution.py
@@ -375,8 +375,8 @@
     shards = don_size * acc_size
     return pl.pallas_call(
         functools.partial(gather_kernel, don_size, acc_size, inner),
-        in_specs=[any_space] * 3,
-        out_specs=[any_space] * 3,
+        in_specs=[pl.BlockSpec(memory_space=pltpu.VMEM), any_space, any_space],
+        out_specs=[pl.BlockSpec(memory_space=pltpu.VMEM), any_space, any_space],
         out_shape=[
             jax.ShapeDtypeStruct((shards,) + x.shape, x.dtype),
             jax.ShapeDtypeStruct((don_size,) + comb.shape, comb.dtype),

time: 67.2 us -> 67.5 us (level)
  no operation moved by 1% of the time
where the time goes in v4:
time: 67.5 us; the launch traced here: 67.1 us
  Pallas kernels  65.2 us (97%)
  local copies, waits for them, and re-layouts  1.19 us (2%)
    pallas_call x1, Pallas kernels, gather(): pl.pallas_call(functools.partial(gather_kernel, don_size, acc_size, inner...  29.6 us
    pallas_call x1, Pallas kernels, compute(): pl.pallas_call(functools.partial(compute_kernel, slots, live), grid=(tiss...  23.6 us
    pallas_call x1, Pallas kernels, loss_sum(): pl.pallas_call(functools.partial(loss_kernel, acc_size), in_specs=[pl.Blo...  8.95 us
    pallas_call x1, Pallas kernels, fetch(): pl.pallas_call(fetch_kernel, in_specs=[smem, smem, hbm, hbm, vmem, vmem],...  3.09 us

profile of v4, /device:TPU:0, one launch (start us, length us, event | category | flops | bytes accessed | tf_op | source)
XLA Modules:
  0.0 67.1 jit_solution(18145742941014249673)
XLA Ops:
  0.6 3.1 %shard_map.104 = (bf16[24,1536]{1,0:T(8,128)(2,1)}, s32[8,192]{1,0:T(8,128)}) custom-call(s32[24]{0:T(128)} %dpos.1, s32[24]{0:T(128)} %apos.1, bf16[2048,768]{1,0:T(8,128)(2,1)} %demb_ref.1, bf16[2048,768]{1,0:T(8,128)(2,1)} %aemb_ref.1, s32[64,192]{1,0:T(8,128)} %target_ref.1, s32[64,192]{1,0:T(8,128)} %mask_ref.1), custom_call_target="tpu_custom_call" | custom-call | tf_op jit(solution)/shard_map/pallas_call | solution.py:230
  3.7 29.6 %shard_map.105 = (bf16[32,24,1536]{2,1,0:T(8,128)(2,1)}, s32[4,8,192]{2,1,0:T(8,128)}, s32[4,1,8]{2,1,0:T(1,128)}) custom-call(bf16[24,1536]{1,0:T(8,128)(2,1)} %get-tuple-element.9.x_ref, s32[8,192]{1,0:T(8,128)} %get-tuple-element.10.comb_ref, s32[1,8]{1,0:T(1,128)} %bitcast.5), custom_call_target="tpu_custom_call" | custom-call | tf_op jit(solution)/shard_map/pallas_call | solution.py:376
  33.3 23.6 %shard_map.106 = (f32[192,8,768]{2,1,0:T(8,128)}, f32[8,128]{1,0:T(8,128)}) custom-call(s32[4,1,8]{2,1,0:T(1,128)} %get-tuple-element.11.dcnt, s32[1,1,32]{2,1,0:T(1,128)} %bitcast.6, bf16[768,1536]{1,0:T(8,128)(2,1)} %bitcast.4, s32[4,8,192]{2,1,0:T(8,128)} %get-tuple-element.13.comb_ref, bf16[8,768,768]{2,1,0:T(8,128)(2,1)} %w_ref.1), custom_call_target="tpu_custom_call" | custom-call | tf_op jit(solution)/shard_map/pallas_call | solution.py:157
  56.9 8.9 %shard_map.107 = f32[8,128]{1,0:T(8,128)} custom-call(f32[8,128]{1,0:T(8,128)} %get-tuple-element.14.sums_ref), custom_call_target="tpu_custom_call" | custom-call | tf_op jit(solution)/shard_map/pallas_call | solution.py:427
  65.9 1.2 %slice.3 = f32[1,1]{1,0:T(1,128)} slice(f32[8,128]{1,0:T(8,128)} %shard_map.107), slice={[0:1], [0:1]} | slice | bytes 8 | tf_op jit(solution)/shard_map/slice | solution.py:463
